TPU v7x, 128 devices: a whole 4x4x4 slice. The times are simulated.
128 devices in a mesh: tok: 16 (over y, z), head: 8 (over x, core).
Axes of the slice: x: 4, y: 4, z: 4, core: 2. Of those that a mesh axis runs over, the one named last changes fastest.
Arguments:
- prefill_states: bfloat16 [4, 2048, 2048], P(None, 'tok'), may hold values from -6 to 6
- decode_states: bfloat16 [128, 2048], P('tok'), may hold values from -6 to 6
- attn_gain: float32 [2048], replicated, may hold values from 0.1 to 1.9
- w_qkv: bfloat16 [2048, 3, 2048], P(None, None, 'head'), may hold values from -0.125 to 0.125
- w_out: bfloat16 [2048, 2048], P('head'), may hold values from -0.125 to 0.125
- ffn_gain: float32 [2048], replicated, may hold values from 0.1 to 1.9
- w_gate_up: bfloat16 [2048, 2, 5120], P(None, None, 'tok'), may hold values from -0.125 to 0.125
- w_down: bfloat16 [5120, 2048], P('tok'), may hold values from -0.078125 to 0.078125
- prefill_pool: bfloat16 [768, 128, 1024], P('tok', None, 'head')
- prefill_pages: int32 [16, 48], P('tok'), may hold values from 0 to 47, as said below
- prefill_lengths: int32 [4], replicated, may hold values from 1 to 6144, as said below
- prefill_home: int32 [16], replicated, may hold values from 0 to 15, each once
- decode_pool: bfloat16 [1024, 128, 4096], P('tok', None, 'head')
- decode_pages: int32 [128, 32], P('tok'), may hold values from 0 to 63, as said below
- decode_lengths: int32 [128], P('tok'), may hold values from 1 to 4096, as said below
- decode_home: int32 [128], replicated, may hold values from 0 to 127, each once
Outputs:
- prefill_out: bfloat16 [4, 2048, 2048], P(None, ('tok', 'head'))
- decode_out: bfloat16 [128, 2048], P(('tok', 'head'))
Inputs may be any that keep to these rules, and one draw needn't show every extreme that they name: `prefill_pages`: each row is an ordering of all 48 pages of the prefill pool on that row's tok index. `prefill_lengths`: one prefill request has exactly 6144 cached tokens. `decode_pages`: slot s lies on tok index s // 8; within one tok index the first ceil(length / 128) pages of its slots are all different. `decode_lengths`: every tok index hosts one decode request of exactly 4096 cached tokens.
All inputs are finite; a program needn't handle non-finite values.
Results may differ from a plain program's by a relative error of at most 0.017.
The roundings to bfloat16 on the way count: a program that leaves them out, or rounds other values in their place, can miss the bound.
Values may be sent and summed in bfloat16 or wider, within the bound.
A program may use at most 128 MiB of HBM per device.

v0:
```python
import math
import jax
import jax.numpy as jnp
from jax import lax
from jax.sharding import PartitionSpec as P

HD = 64
EPSILON = 1e-06
SCALE = 0.125
MASKED = -1e30


def rms_norm(rows, gain):
    values = rows.astype(jnp.float32)
    inverse = lax.rsqrt(jnp.mean(values * values, axis=-1, keepdims=True) + EPSILON)
    return (values * inverse * gain).astype(jnp.bfloat16)


def inner(left, right):
    return lax.dot_general(
        left, right, (((1,), (1,)), ((), ())), preferred_element_type=jnp.float32
    )


def shards(
    prefill_states,
    decode_states,
    attn_gain,
    w_qkv,
    w_out,
    ffn_gain,
    w_gate_up,
    w_down,
    prefill_pool,
    prefill_pages,
    prefill_lengths,
    prefill_home,
    decode_pool,
    decode_pages,
    decode_lengths,
    decode_home,
):
    n_tok = lax.axis_size("tok")
    n_head = lax.axis_size("head")
    my_tok = lax.axis_index("tok")
    my_head = lax.axis_index("head")
    requests, positions, width = prefill_states.shape
    hosted = decode_states.shape[0]
    heads_per = w_qkv.shape[2] // HD
    stretch = positions * n_tok
    units = requests * heads_per
    features = heads_per * HD
    normed_pre = rms_norm(prefill_states, attn_gain).reshape(requests * positions, width)
    normed_dec = rms_norm(decode_states, attn_gain)
    normed = jnp.concatenate([normed_pre, normed_dec], axis=0)
    projected = jnp.dot(
        normed, w_qkv.reshape(width, 3 * features), preferred_element_type=jnp.float32
    ).astype(jnp.bfloat16)
    proj_pre = projected[: requests * positions].reshape(requests, positions, 3, heads_per, HD)
    proj_dec = projected[requests * positions :]
    unit_ids = jnp.arange(units, dtype=jnp.int32)
    host_ids = jnp.arange(n_tok, dtype=jnp.int32)
    hosted_unit = jnp.sum(
        jnp.where(prefill_home[None, :] == host_ids[:, None], unit_ids[None, :], 0), axis=1
    )
    by_unit = jnp.transpose(proj_pre, (0, 3, 1, 2, 4)).reshape(units, positions * 3 * HD)
    outgoing = jnp.take(by_unit, hosted_unit, axis=0)
    pre_cols = positions * 3 * HD
    spread = jnp.broadcast_to(
        proj_dec.reshape(1, hosted * 3 * features), (n_tok, hosted * 3 * features)
    )
    outgoing = jnp.concatenate([outgoing, spread], axis=1)
    arrived = lax.all_to_all(outgoing, "tok", split_axis=0, concat_axis=0, tiled=True)
    arrived_dec = arrived[:, pre_cols:].reshape(n_tok * hosted, 3, heads_per, HD)
    arrived_pre = arrived[:, :pre_cols].reshape(stretch, 3, HD)
    query_rows = arrived_pre[:, 0]
    key_rows = arrived_pre[:, 1]
    value_rows = arrived_pre[:, 2]
    my_unit = hosted_unit[my_tok]
    length = prefill_lengths[my_unit // heads_per]
    cache = jnp.take(prefill_pool, prefill_pages[0], axis=0).reshape(-1, 2 * HD)
    cache_keys = cache[:, :HD]
    cache_values = cache[:, HD:]
    span = cache.shape[0]
    block = math.gcd(stretch, 512)

    def attend(start):
        rows = lax.dynamic_slice_in_dim(query_rows, start, block, 0)
        score_cache = inner(rows, cache_keys) * SCALE
        score_cache = jnp.where(jnp.arange(span)[None, :] < length, score_cache, MASKED)
        score_stretch = inner(rows, key_rows) * SCALE
        row_pos = start + jnp.arange(block)[:, None]
        score_stretch = jnp.where(jnp.arange(stretch)[None, :] <= row_pos, score_stretch, MASKED)
        top = jnp.maximum(
            jnp.max(score_cache, axis=1, keepdims=True),
            jnp.max(score_stretch, axis=1, keepdims=True),
        )
        weight_cache = jnp.exp(score_cache - top)
        weight_stretch = jnp.exp(score_stretch - top)
        total = jnp.sum(weight_cache, axis=1, keepdims=True) + jnp.sum(
            weight_stretch, axis=1, keepdims=True
        )
        mixed = jnp.dot(
            weight_cache.astype(jnp.bfloat16), cache_values, preferred_element_type=jnp.float32
        )
        mixed = mixed + jnp.dot(
            weight_stretch.astype(jnp.bfloat16), value_rows, preferred_element_type=jnp.float32
        )
        return (mixed / total).astype(jnp.bfloat16)

    starts = jnp.arange(stretch // block, dtype=jnp.int32) * block
    attn_unit = lax.map(attend, starts).reshape(stretch, HD)
    slots = my_tok * hosted + jnp.arange(hosted, dtype=jnp.int32)
    all_requests = jnp.arange(decode_home.shape[0], dtype=jnp.int32)
    anchor = jnp.sum(
        jnp.where(decode_home[None, :] == slots[:, None], all_requests[None, :], 0), axis=1
    )
    mine = jnp.take(arrived_dec, anchor, axis=0)

    def decode_one(operands):
        pages, slot_length, rows = operands
        cache_slot = jnp.take(decode_pool, pages, axis=0).reshape(-1, heads_per, 2 * HD)
        query = rows[0]
        scores = (
            jnp.einsum(
                "hd,khd->hk", query, cache_slot[:, :, :HD], preferred_element_type=jnp.float32
            )
            * SCALE
        )
        scores = jnp.where(jnp.arange(cache_slot.shape[0])[None, :] < slot_length, scores, MASKED)
        own_score = (
            jnp.sum(query.astype(jnp.float32) * rows[1].astype(jnp.float32), axis=1, keepdims=True)
            * SCALE
        )
        top = jnp.maximum(jnp.max(scores, axis=1, keepdims=True), own_score)
        weights = jnp.exp(scores - top)
        own_weight = jnp.exp(own_score - top)
        total = jnp.sum(weights, axis=1, keepdims=True) + own_weight
        mixed = jnp.einsum(
            "hk,khd->hd",
            weights.astype(jnp.bfloat16),
            cache_slot[:, :, HD:],
            preferred_element_type=jnp.float32,
        )
        mixed = mixed + own_weight.astype(jnp.bfloat16).astype(jnp.float32) * rows[2].astype(
            jnp.float32
        )
        return (mixed / total).astype(jnp.bfloat16).reshape(features)

    decode_attn = lax.map(decode_one, (decode_pages, decode_lengths, mine))
    backward = attn_unit.reshape(n_tok, positions * HD)
    back_cols = positions * HD
    spread_back = jnp.broadcast_to(
        decode_attn.reshape(1, hosted * features), (n_tok, hosted * features)
    )
    backward = jnp.concatenate([backward, spread_back], axis=1)
    returned = lax.all_to_all(backward, "tok", split_axis=0, concat_axis=0, tiled=True)
    by_slot = returned[:, back_cols:].reshape(n_tok * hosted, features)
    my_slots = lax.dynamic_slice_in_dim(decode_home, my_tok * hosted, hosted, 0)
    attn_dec = jnp.take(by_slot, my_slots, axis=0)
    attn_pre = jnp.take(returned[:, :back_cols], prefill_home, axis=0).reshape(
        requests, heads_per, positions, HD
    )
    block_rows = positions // n_head
    decode_share = hosted // n_head
    per = requests * block_rows + decode_share
    pre_rows = jnp.transpose(attn_pre, (0, 2, 1, 3)).reshape(requests, n_head, block_rows, features)
    pre_rows = jnp.transpose(pre_rows, (1, 0, 2, 3)).reshape(
        n_head, requests * block_rows, features
    )
    dec_rows = attn_dec.reshape(n_head, decode_share, features)
    ordered = jnp.concatenate([pre_rows, dec_rows], axis=1).reshape(n_head * per, features)
    mixed_rows = lax.psum_scatter(
        jnp.dot(ordered, w_out, preferred_element_type=jnp.float32).astype(jnp.bfloat16),
        "head",
        scatter_dimension=0,
        tiled=True,
    ).astype(jnp.float32)
    own_pre = lax.dynamic_slice_in_dim(prefill_states, my_head * block_rows, block_rows, 1).reshape(
        requests * block_rows, width
    )
    own_dec = lax.dynamic_slice_in_dim(decode_states, my_head * decode_share, decode_share, 0)
    resid = jnp.concatenate([own_pre, own_dec], axis=0).astype(jnp.float32) + mixed_rows
    normed_mid = rms_norm(resid, ffn_gain)
    piece = lax.all_gather(normed_mid, "tok", axis=0, tiled=True)
    gate = jnp.dot(piece, w_gate_up[:, 0], preferred_element_type=jnp.float32)
    upper = jnp.dot(piece, w_gate_up[:, 1], preferred_element_type=jnp.float32)
    hidden = (jax.nn.gelu(gate, approximate=True) * upper).astype(jnp.bfloat16)
    summed = lax.psum(
        jnp.dot(hidden, w_down, preferred_element_type=jnp.float32).astype(jnp.bfloat16), "tok"
    ).astype(jnp.float32)
    ffn_rows = lax.dynamic_slice_in_dim(summed, my_tok * per, per, 0)
    result = (resid + ffn_rows).astype(jnp.bfloat16)
    prefill_out = result[: requests * block_rows].reshape(requests, block_rows, width)
    decode_out = result[requests * block_rows :]
    return (prefill_out, decode_out)


def solution(mesh):
    placed = (
        P(None, "tok", None),
        P("tok", None),
        P(),
        P(None, None, "head"),
        P("head", None),
        P(),
        P(None, None, "tok"),
        P("tok", None),
        P("tok", None, "head"),
        P("tok", None),
        P(),
        P(),
        P("tok", None, "head"),
        P("tok", None),
        P("tok"),
        P(),
    )
    return jax.shard_map(
        shards,
        mesh=mesh,
        in_specs=placed,
        out_specs=(P(None, ("tok", "head"), None), P(("tok", "head"), None)),
        check_vma=False,
    )
```

profile of v0, /device:TPU:1, one launch (start us, length us, event | category | flops | bytes accessed | tf_op | source)
XLA Modules:
  0.0 700.8 jit_solution(3987301994790291985)
XLA Ops:
  16.1 4.7 copy.74
  20.8 4.4 fusion.67
  36.3 9.1 %all-to-all-start = ((bf16[16,2,15360]{2,1,0:T(2,128)(2,1)}), bf16[16,2,15360]{2,1,0:T(2,128)(2,1)}, u32[]{:S(2)}, u32[]{:S(2)}) async-start(bf16[16,2,15360]{2,1,0:T(2,128)(2,1)} %reshape.373), calls=%async_computation | async-start | bytes 1966080 | tf_op jit(solution)/shard_map/all_to_all | solution.py:73
  61.6 4.2 reshape.374
  67.5 310.7 %while.21 = (s32[]{:T(128)}, bf16[8,256]{1,0:T(8,128)(2,1)S(1)}, s32[8]{0:T(128)S(1)}, bf16[8,3,4,64]{3,2,1,0:T(4,128)(2,1)S(1)}, s32[8,32]{1,0:T(8,128)}, /*ind...) while((s32[]{:T(128)}, bf16[8,256]{1,0:T(8,128)(2,1)S(1)}, s32[8]{0:T(128)S(1)}, ...), condition=%wide.region_14.15_spmd, body=%wide.region_10.14_spmd.sunk | while | flops 6430264 | bytes 38044244 | solution.py:150
  70.4 6.1 gather_fusion
  76.6 6.9 gather.55
  83.5 16.5 %broadcast_select_fusion.4 = bf16[4096,4,128]{2,1,0:T(4,128)(2,1)S(1)} fusion(bf16[4096,4,128]{2,1,0:T(4,128)(2,1)} %gather.55, pred[4096]{0:T(1024)(128)(4,1)S(1)} %broadcast_bitcast_fusion.3), kind=kLoop, calls=%fused_computation.38.clone.1 | loop fusion | flops 2097152 | bytes 8392704 | tf_op jit(solution)/shard_map/while/body/eval_jaxpr/jit(_take)/select_n | solution.py:122
  100.0 3.8 fusion.145
  109.3 6.1 gather_fusion
  115.4 6.9 gather.55
  122.3 16.5 %broadcast_select_fusion.4 = bf16[4096,4,128]{2,1,0:T(4,128)(2,1)S(1)} fusion(bf16[4096,4,128]{2,1,0:T(4,128)(2,1)} %gather.55, pred[4096]{0:T(1024)(128)(4,1)S(1)} %broadcast_bitcast_fusion.3), kind=kLoop, calls=%fused_computation.38.clone.1 | loop fusion | flops 2097152 | bytes 8392704 | tf_op jit(solution)/shard_map/while/body/eval_jaxpr/jit(_take)/select_n | solution.py:122
  138.8 3.8 fusion.145
  148.1 6.1 gather_fusion
  154.2 6.9 gather.55
  161.2 16.5 %broadcast_select_fusion.4 = bf16[4096,4,128]{2,1,0:T(4,128)(2,1)S(1)} fusion(bf16[4096,4,128]{2,1,0:T(4,128)(2,1)} %gather.55, pred[4096]{0:T(1024)(128)(4,1)S(1)} %broadcast_bitcast_fusion.3), kind=kLoop, calls=%fused_computation.38.clone.1 | loop fusion | flops 2097152 | bytes 8392704 | tf_op jit(solution)/shard_map/while/body/eval_jaxpr/jit(_take)/select_n | solution.py:122
  177.6 3.8 fusion.145
  187.0 6.1 gather_fusion
  193.1 6.9 gather.55
  200.0 16.5 %broadcast_select_fusion.4 = bf16[4096,4,128]{2,1,0:T(4,128)(2,1)S(1)} fusion(bf16[4096,4,128]{2,1,0:T(4,128)(2,1)} %gather.55, pred[4096]{0:T(1024)(128)(4,1)S(1)} %broadcast_bitcast_fusion.3), kind=kLoop, calls=%fused_computation.38.clone.1 | loop fusion | flops 2097152 | bytes 8392704 | tf_op jit(solution)/shard_map/while/body/eval_jaxpr/jit(_take)/select_n | solution.py:122
  216.5 3.8 fusion.145
  225.8 6.1 gather_fusion
  231.9 6.9 gather.55
  238.8 16.5 %broadcast_select_fusion.4 = bf16[4096,4,128]{2,1,0:T(4,128)(2,1)S(1)} fusion(bf16[4096,4,128]{2,1,0:T(4,128)(2,1)} %gather.55, pred[4096]{0:T(1024)(128)(4,1)S(1)} %broadcast_bitcast_fusion.3), kind=kLoop, calls=%fused_computation.38.clone.1 | loop fusion | flops 2097152 | bytes 8392704 | tf_op jit(solution)/shard_map/while/body/eval_jaxpr/jit(_take)/select_n | solution.py:122
  255.3 3.8 fusion.145
  264.6 6.1 gather_fusion
  270.7 6.9 gather.55
  277.7 16.5 %broadcast_select_fusion.4 = bf16[4096,4,128]{2,1,0:T(4,128)(2,1)S(1)} fusion(bf16[4096,4,128]{2,1,0:T(4,128)(2,1)} %gather.55, pred[4096]{0:T(1024)(128)(4,1)S(1)} %broadcast_bitcast_fusion.3), kind=kLoop, calls=%fused_computation.38.clone.1 | loop fusion | flops 2097152 | bytes 8392704 | tf_op jit(solution)/shard_map/while/body/eval_jaxpr/jit(_take)/select_n | solution.py:122
  303.5 6.1 gather_fusion
  309.6 6.9 gather.55
  316.5 16.5 %broadcast_select_fusion.4 = bf16[4096,4,128]{2,1,0:T(4,128)(2,1)S(1)} fusion(bf16[4096,4,128]{2,1,0:T(4,128)(2,1)} %gather.55, pred[4096]{0:T(1024)(128)(4,1)S(1)} %broadcast_bitcast_fusion.3), kind=kLoop, calls=%fused_computation.38.clone.1 | loop fusion | flops 2097152 | bytes 8392704 | tf_op jit(solution)/shard_map/while/body/eval_jaxpr/jit(_take)/select_n | solution.py:122
  333.0 3.8 fusion.145
  342.3 6.1 gather_fusion
  348.4 6.9 gather.55
  355.3 16.5 %broadcast_select_fusion.4 = bf16[4096,4,128]{2,1,0:T(4,128)(2,1)S(1)} fusion(bf16[4096,4,128]{2,1,0:T(4,128)(2,1)} %gather.55, pred[4096]{0:T(1024)(128)(4,1)S(1)} %broadcast_bitcast_fusion.3), kind=kLoop, calls=%fused_computation.38.clone.1 | loop fusion | flops 2097152 | bytes 8392704 | tf_op jit(solution)/shard_map/while/body/eval_jaxpr/jit(_take)/select_n | solution.py:122
  384.0 76.3 %while.20 = (s32[]{:T(128)}, bf16[4,512,64]{1,2,0:T(8,128)(2,1)}, s32[]{:T(128)}, s32[4]{0:T(128)}, bf16[2048,64]{1,0:T(8,128)(2,1)S(1)}, /*index=5*/bf16[6144,6...) while((s32[]{:T(128)}, bf16[4,512,64]{1,2,0:T(8,128)(2,1)}, ...), condition=%wide.region_8.9_spmd, body=%wide.region_3.8_spmd.sunk | while | flops 1116837376 | bytes 57026836 | solution.py:112
  397.3 4.3 fusion.136
  416.4 4.3 fusion.136
  435.4 4.3 fusion.136
  454.4 4.3 fusion.136
  464.6 6.8 all-to-all-start.1
  473.0 6.1 all-to-all-done.1
  485.0 21.3 %fusion = bf16[72,2048]{1,0:T(8,128)(2,1)S(1)} fusion(bf16[520,2048]{1,0:T(8,128)(2,1)S(1)} %convolution_convert_fusion.1), kind=kCustom, calls=%all-reduce-scatter | all-reduce-scatter fusion | flops 1179649 | bytes 2425344
  514.9 52.3 %all-gather.3.cloned.1.call-done = bf16[16,65,2048]{2,1,0:T(8,128)(2,1)} async-done(((bf16[1,65,2048]{2,1,0:T(8,128)(2,1)}), bf16[16,65,2048]{2,1,0:T(8,128)(2,1)}) %all-gather.3.cloned.1.call-update) | async-done | bytes 4259856 | tf_op jit(solution)/shard_map/all_gather | solution.py:185
  567.1 4.4 reshape.365
  571.6 5.6 fusion.71
  577.2 10.4 %convolution_convert_fusion = bf16[1040,2048]{1,0:T(8,128)(2,1)} fusion(bf16[320,2048]{1,0:T(8,128)(2,1)} %param.27, bf16[1040,2048]{1,0:T(8,128)(2,1)} %reshape.365, f32[1040,320]{0,1:T(8,128)} %fusion.71, bf16[2048,2,320]{0,2,1:T(8,128)(2,1)} %param.26), kind=kOutput, calls=%fused_computation.70 | convolution fusion | flops 2731755520 | bytes 12615680 | tf_op jit(solution)/shard_map/dot_general | solution.py:190
  587.6 103.6 %all-reduce.4.cloned.1.call-done = bf16[1040,2048]{1,0:T(8,128)(2,1)} async-done(((bf16[1040,2048]{1,0:T(8,128)(2,1)}), bf16[1040,2048]{1,0:T(8,128)(2,1)}) %all-reduce.4.cloned.1.call-update) | async-done | bytes 4259856 | tf_op jit(solution)/shard_map/psum | solution.py:189
  (320 shorter events, 165.7 us)
Async XLA Ops:
  7.2 48.0 %copy-start = (bf16[48,128,128]{2,1,0:T(8,128)(2,1)S(1)}, bf16[48,128,128]{2,1,0:T(8,128)(2,1)}, u32[]{:S(2)}) copy-start(bf16[48,128,128]{2,1,0:T(8,128)(2,1)} %param.28) | copy-start | bytes 4718596
  8.1 12.7 %copy-start.11 = (s32[16]{0:T(128)}, s32[16]{0:T(128)S(1)}, u32[]{:S(2)}) copy-start(s32[16]{0:T(128)S(1)} %select_reduce_fusion) | copy-start | bytes 196
  32.4 17.1 %copy-start.9 = (s32[16]{0:T(128)S(1)}, s32[16]{0:T(128)}, u32[]{:S(2)}) copy-start(s32[16]{0:T(128)} %param.31) | copy-start | bytes 196
  32.4 18.2 %copy-start.10 = (s32[128]{0:T(128)S(1)}, s32[128]{0:T(128)}, u32[]{:S(2)}) copy-start(s32[128]{0:T(128)} %param.35) | copy-start | bytes 1540
  32.5 20.4 %copy-start.8 = (u32[128]{0:T(128)S(1)}, u32[128]{0:T(128)}, u32[]{:S(2)}) copy-start(u32[128]{0:T(128)} %constant.188) | copy-start | bytes 1540
  36.3 25.3 %all-to-all-start = ((bf16[16,2,15360]{2,1,0:T(2,128)(2,1)}), bf16[16,2,15360]{2,1,0:T(2,128)(2,1)}, u32[]{:S(2)}, u32[]{:S(2)}) async-start(bf16[16,2,15360]{2,1,0:T(2,128)(2,1)} %reshape.373), calls=%async_computation | async-start | bytes 1966080 | tf_op jit(solution)/shard_map/all_to_all | solution.py:73
  61.6 5.9 copy-start.12
  387.3 3.3 copy-start.2
  397.3 4.3 copy-start.3
  397.3 4.3 copy-start.4
  406.4 3.3 copy-start.2
  416.4 4.3 copy-start.3
  416.4 4.3 copy-start.4
  425.4 3.3 copy-start.2
  435.4 4.3 copy-start.3
  435.4 4.3 copy-start.4
  444.4 3.3 copy-start.2
  454.4 4.3 copy-start.3
  454.4 4.3 copy-start.4
  460.3 20.2 %copy-start.6 = (pred[8]{0:T(512)(128)(4,1)S(1)}, pred[8]{0:T(512)(128)(4,1)}, u32[]{:S(2)}) copy-start(pred[8]{0:T(512)(128)(4,1)} %get-tuple-element.149) | copy-start | bytes 28
  462.8 19.2 %copy-start.7 = (pred[4,4]{1,0:T(4,128)(4,1)S(1)}, pred[4,4]{1,0:T(4,128)(4,1)}, u32[]{:S(2)}) copy-start(pred[4,4]{1,0:T(4,128)(4,1)} %broadcast_in_dim.177) | copy-start | bytes 52
  464.6 14.6 %all-to-all-start.1 = ((bf16[16,2,5120]{2,1,0:T(2,128)(2,1)}), bf16[16,2,5120]{2,1,0:T(2,128)(2,1)S(1)}, u32[]{:S(2)}, u32[]{:S(2)}) async-start(bf16[16,2,5120]{2,1,0:T(2,128)(2,1)} %reshape.375), calls=%async_computation.1 | async-start | bytes 655360 | tf_op jit(solution)/shard_map/all_to_all | solution.py:157
  471.3 95.8 %all-gather.3.cloned.1.call-start = ((), (), s32[]{:S(2)}) async-start(), calls=%async_computation.3 | async-start | bytes 5013504 | tf_op jit(solution)/shard_map/all_gather | solution.py:185
  483.0 30.9 %copy-start.5 = (f32[2048]{0:T(1024)S(1)}, f32[2048]{0:T(1024)}, u32[]{:S(2)}) copy-start(f32[2048]{0:T(1024)} %param.25) | copy-start | bytes 24580
  506.3 6.8 collective-permute-start
  514.8 176.4 %all-reduce.4.cloned.1.call-start = ((), (), s32[]{:S(2)}) async-start(), calls=%async_computation.2 | async-start | bytes 8519680 | tf_op jit(solution)/shard_map/psum | solution.py:189
  577.2 116.5 %copy-start.1 = (bf16[48,128,128]{2,1,0:T(8,128)(2,1)S(1)}, bf16[48,128,128]{2,1,0:T(8,128)(2,1)}, u32[]{:S(2)}) copy-start(bf16[48,128,128]{2,1,0:T(8,128)(2,1)} %param.28) | copy-start | bytes 4718596
Sparse Core Ops, SparseCore 0:
  514.9 52.1 all-gather.2
  587.8 103.4 all-reduce.3
where the time goes:
time: 710 us; the launch traced here: 701 us
  other arithmetic  200 us (28%)
  local copies, waits for them, and re-layouts  193 us (27%)
  waiting for transfers between devices  164 us (23%)
  matrix products  76.3 us (11%)
  blocking collectives  21.3 us (3%)
  starting transfers between devices  19.8 us (3%)
  between operations  17.5 us (2%)
  loops' own time  8.49 us (1%)
    select_n x16, other arithmetic, decode_one(): jnp.take(decode_pool, pages, axis=0).reshape(-1, heads_per, 2 * HD)  137 us
    gather x16, local copies, waits for them, and re-layouts, decode_one(): jnp.take(decode_pool, pages, axis=0).reshape(-1, heads_per, 2 * HD)  104 us
    psum x1, waiting for transfers between devices, shards(): lax.psum(jnp.dot(hidden, w_down, preferred_element_type=jnp.float32).asty...  104 us
    all_gather x1, waiting for transfers between devices, shards(): piece = lax.all_gather(normed_mid, 'tok', axis=0, tiled=True)  52.3 us
    slice x8, local copies, waits for them, and re-layouts, decode_one(): cache_slot[:, :, :HD]  30.5 us
    unnamed x1, blocking collectives  21.3 us
    unnamed x32, local copies, waits for them, and re-layouts  18.4 us
    dot_general x4, matrix products, attend(): jnp.dot(weight_cache.astype(jnp.bfloat16), cache_values, preferred_elemen...  17.3 us
  transfers between devices with their start and end apart: 5, of which 4 were waited for; matrix products, arithmetic and copies ran while one was open for 2% of the time, Pallas kernels for 0%

commit v1 on v0

--- a/solution.py
+++ b/solution.py
@@ -186,8 +186,11 @@
     gate = jnp.dot(piece, w_gate_up[:, 0], preferred_element_type=jnp.float32)
     upper = jnp.dot(piece, w_gate_up[:, 1], preferred_element_type=jnp.float32)
     hidden = (jax.nn.gelu(gate, approximate=True) * upper).astype(jnp.bfloat16)
-    summed = lax.psum(
-        jnp.dot(hidden, w_down, preferred_element_type=jnp.float32).astype(jnp.bfloat16), "tok"
+    summed = jnp.sum(
+        lax.all_gather(
+            jnp.dot(hidden, w_down, preferred_element_type=jnp.float32).astype(jnp.bfloat16), "tok"
+        ),
+        axis=0,
     ).astype(jnp.float32)
     ffn_rows = lax.dynamic_slice_in_dim(summed, my_tok * per, per, 0)
     result = (resid + ffn_rows).astype(jnp.bfloat16)

time: 710 us -> 1000 us (1.41)
  waiting for transfers between devices: 164 us -> 434 us
  other arithmetic: 200 us -> 224 us
    all_gather x0 -> x1, waiting for transfers between devices: none -> 374 us  [shards(): lax.all_gather(jnp.dot(hidden, w_down, preferred_element_type=jnp.float32...]
    psum x1 -> x0, waiting for transfers between devices: 104 us -> none  [shards(): lax.psum(jnp.dot(hidden, w_down, preferred_element_type=jnp.float32).asty...]
    reduce_sum x0 -> x1, other arithmetic: none -> 24.6 us  [shards(): jnp.sum(lax.all_gather(jnp.dot(hidden, w_down, preferred_element_type=jnp...]
where the time goes in v1:
time: 1000 us; the launch traced here: 995 us
  waiting for transfers between devices  434 us (43%)
  other arithmetic  224 us (22%)
  local copies, waits for them, and re-layouts  193 us (19%)
  matrix products  76 us (8%)
  blocking collectives  21.3 us (2%)
  starting transfers between devices  19.8 us (2%)
  between operations  17.5 us (2%)
    all_gather x1, waiting for transfers between devices, shards(): lax.all_gather(jnp.dot(hidden, w_down, preferred_element_type=jnp.float32...  374 us
    select_n x16, other arithmetic, decode_one(): jnp.take(decode_pool, pages, axis=0).reshape(-1, heads_per, 2 * HD)  137 us
    gather x16, local copies, waits for them, and re-layouts, decode_one(): jnp.take(decode_pool, pages, axis=0).reshape(-1, heads_per, 2 * HD)  104 us
    all_gather x1, waiting for transfers between devices, shards(): piece = lax.all_gather(normed_mid, 'tok', axis=0, tiled=True)  52.3 us
    slice x8, local copies, waits for them, and re-layouts, decode_one(): cache_slot[:, :, :HD]  30.5 us
    reduce_sum x1, other arithmetic, shards(): jnp.sum(lax.all_gather(jnp.dot(hidden, w_down, preferred_element_type=jnp...  24.6 us
    unnamed x1, blocking collectives  21.3 us
  transfers between devices with their start and end apart: 5, of which 4 were waited for; matrix products, arithmetic and copies ran while one was open for 2% of the time, Pallas kernels for 0%

profile of v1, /device:TPU:1, one launch (start us, length us, event | category | flops | bytes accessed | tf_op | source)
XLA Modules:
  0.0 995.2 jit_solution(10285119599671011633)
XLA Ops:
  16.1 4.7 copy.74
  20.8 4.4 fusion.67
  36.3 9.1 all-to-all-start
  61.6 4.2 reshape.375
  67.5 310.7 %while.21 = (s32[]{:T(128)}, bf16[8,256]{1,0:T(8,128)(2,1)S(1)}, s32[8]{0:T(128)S(1)}, bf16[8,3,4,64]{3,2,1,0:T(4,128)(2,1)S(1)}, s32[8,32]{1,0:T(8,128)}, /*ind...) while((s32[]{:T(128)}, bf16[8,256]{1,0:T(8,128)(2,1)S(1)}, s32[8]{0:T(128)S(1)}, ...), condition=%wide.region_14.15_spmd, body=%wide.region_10.14_spmd.sunk | while | flops 6430264 | bytes 38044244 | solution.py:150
  70.4 6.1 gather_fusion
  76.6 6.9 gather.55
  83.5 16.5 %broadcast_select_fusion.4 = bf16[4096,4,128]{2,1,0:T(4,128)(2,1)S(1)} fusion(bf16[4096,4,128]{2,1,0:T(4,128)(2,1)} %gather.55, pred[4096]{0:T(1024)(128)(4,1)S(1)} %broadcast_bitcast_fusion.3), kind=kLoop, calls=%fused_computation.38.clone.1 | loop fusion | flops 2097152 | bytes 8392704 | tf_op jit(solution)/shard_map/while/body/eval_jaxpr/jit(_take)/select_n | solution.py:122
  100.0 3.8 fusion.145
  109.3 6.1 gather_fusion
  115.4 6.9 gather.55
  122.3 16.5 %broadcast_select_fusion.4 = bf16[4096,4,128]{2,1,0:T(4,128)(2,1)S(1)} fusion(bf16[4096,4,128]{2,1,0:T(4,128)(2,1)} %gather.55, pred[4096]{0:T(1024)(128)(4,1)S(1)} %broadcast_bitcast_fusion.3), kind=kLoop, calls=%fused_computation.38.clone.1 | loop fusion | flops 2097152 | bytes 8392704 | tf_op jit(solution)/shard_map/while/body/eval_jaxpr/jit(_take)/select_n | solution.py:122
  138.8 3.8 fusion.145
  148.1 6.1 gather_fusion
  154.2 6.9 gather.55
  161.2 16.5 %broadcast_select_fusion.4 = bf16[4096,4,128]{2,1,0:T(4,128)(2,1)S(1)} fusion(bf16[4096,4,128]{2,1,0:T(4,128)(2,1)} %gather.55, pred[4096]{0:T(1024)(128)(4,1)S(1)} %broadcast_bitcast_fusion.3), kind=kLoop, calls=%fused_computation.38.clone.1 | loop fusion | flops 2097152 | bytes 8392704 | tf_op jit(solution)/shard_map/while/body/eval_jaxpr/jit(_take)/select_n | solution.py:122
  177.6 3.8 fusion.145
  187.0 6.1 gather_fusion
  193.1 6.9 gather.55
  200.0 16.5 %broadcast_select_fusion.4 = bf16[4096,4,128]{2,1,0:T(4,128)(2,1)S(1)} fusion(bf16[4096,4,128]{2,1,0:T(4,128)(2,1)} %gather.55, pred[4096]{0:T(1024)(128)(4,1)S(1)} %broadcast_bitcast_fusion.3), kind=kLoop, calls=%fused_computation.38.clone.1 | loop fusion | flops 2097152 | bytes 8392704 | tf_op jit(solution)/shard_map/while/body/eval_jaxpr/jit(_take)/select_n | solution.py:122
  225.8 6.1 gather_fusion
  231.9 6.9 gather.55
  238.8 16.5 %broadcast_select_fusion.4 = bf16[4096,4,128]{2,1,0:T(4,128)(2,1)S(1)} fusion(bf16[4096,4,128]{2,1,0:T(4,128)(2,1)} %gather.55, pred[4096]{0:T(1024)(128)(4,1)S(1)} %broadcast_bitcast_fusion.3), kind=kLoop, calls=%fused_computation.38.clone.1 | loop fusion | flops 2097152 | bytes 8392704 | tf_op jit(solution)/shard_map/while/body/eval_jaxpr/jit(_take)/select_n | solution.py:122
  255.3 3.8 fusion.145
  264.6 6.1 gather_fusion
  270.7 6.9 gather.55
  277.7 16.5 %broadcast_select_fusion.4 = bf16[4096,4,128]{2,1,0:T(4,128)(2,1)S(1)} fusion(bf16[4096,4,128]{2,1,0:T(4,128)(2,1)} %gather.55, pred[4096]{0:T(1024)(128)(4,1)S(1)} %broadcast_bitcast_fusion.3), kind=kLoop, calls=%fused_computation.38.clone.1 | loop fusion | flops 2097152 | bytes 8392704 | tf_op jit(solution)/shard_map/while/body/eval_jaxpr/jit(_take)/select_n | solution.py:122
  303.5 6.1 gather_fusion
  309.6 6.9 gather.55
  316.5 16.5 %broadcast_select_fusion.4 = bf16[4096,4,128]{2,1,0:T(4,128)(2,1)S(1)} fusion(bf16[4096,4,128]{2,1,0:T(4,128)(2,1)} %gather.55, pred[4096]{0:T(1024)(128)(4,1)S(1)} %broadcast_bitcast_fusion.3), kind=kLoop, calls=%fused_computation.38.clone.1 | loop fusion | flops 2097152 | bytes 8392704 | tf_op jit(solution)/shard_map/while/body/eval_jaxpr/jit(_take)/select_n | solution.py:122
  333.0 3.8 fusion.145
  342.3 6.1 gather_fusion
  348.4 6.9 gather.55
  355.3 16.5 %broadcast_select_fusion.4 = bf16[4096,4,128]{2,1,0:T(4,128)(2,1)S(1)} fusion(bf16[4096,4,128]{2,1,0:T(4,128)(2,1)} %gather.55, pred[4096]{0:T(1024)(128)(4,1)S(1)} %broadcast_bitcast_fusion.3), kind=kLoop, calls=%fused_computation.38.clone.1 | loop fusion | flops 2097152 | bytes 8392704 | tf_op jit(solution)/shard_map/while/body/eval_jaxpr/jit(_take)/select_n | solution.py:122
  384.0 76.3 %while.20 = (s32[]{:T(128)}, bf16[4,512,64]{1,2,0:T(8,128)(2,1)}, s32[]{:T(128)}, s32[4]{0:T(128)}, bf16[2048,64]{1,0:T(8,128)(2,1)S(1)}, /*index=5*/bf16[6144,6...) while((s32[]{:T(128)}, bf16[4,512,64]{1,2,0:T(8,128)(2,1)}, ...), condition=%wide.region_8.9_spmd, body=%wide.region_3.8_spmd.sunk | while | flops 1116837376 | bytes 57026836 | solution.py:112
  397.3 4.3 fusion.136
  416.4 4.3 fusion.136
  435.4 4.3 fusion.136
  454.4 4.3 fusion.136
  464.6 6.8 all-to-all-start.1
  473.0 6.1 all-to-all-done.1
  485.0 21.3 %fusion = bf16[72,2048]{1,0:T(8,128)(2,1)S(1)} fusion(bf16[520,2048]{1,0:T(8,128)(2,1)S(1)} %convolution_convert_fusion.1), kind=kCustom, calls=%all-reduce-scatter | all-reduce-scatter fusion | flops 1179649 | bytes 2425344
  514.9 52.3 %all-gather.7.cloned.1.call-done = bf16[16,65,2048]{2,1,0:T(8,128)(2,1)} async-done(((bf16[1,65,2048]{2,1,0:T(8,128)(2,1)}), bf16[16,65,2048]{2,1,0:T(8,128)(2,1)}) %all-gather.7.cloned.1.call-update) | async-done | bytes 4259856 | tf_op jit(solution)/shard_map/all_gather | solution.py:185
  567.1 4.4 reshape.366
  571.6 5.7 fusion.71
  577.3 10.0 %convolution_convert_fusion = bf16[1040,2048]{1,0:T(8,128)(2,1)} fusion(bf16[320,2048]{1,0:T(8,128)(2,1)S(1)} %copy-done.12, bf16[1040,2048]{1,0:T(8,128)(2,1)} %reshape.366, f32[1040,320]{0,1:T(8,128)} %fusion.71, bf16[2048,2,320]{0,2,1:T(8,128)(2,1)} %param.26), kind=kOutput, calls=%fused_computation.70 | convolution fusion | flops 2731755520 | bytes 12615680 | tf_op jit(solution)/shard_map/dot_general | solution.py:191
  587.3 373.8 %all-gather.5.cloned.1.call-done = bf16[16640,2048]{1,0:T(8,128)(2,1)} async-done(((bf16[1040,2048]{1,0:T(8,128)(2,1)}), bf16[16640,2048]{1,0:T(8,128)(2,1)}) %all-gather.5.cloned.1.call-update) | async-done | bytes 68157456 | tf_op jit(solution)/shard_map/all_gather | solution.py:190
  961.1 24.6 %reduce_sum.104 = bf16[1040,2048]{1,0:T(8,128)(2,1)} reduce(bf16[16,1040,2048]{2,1,0:T(8,128)(2,1)} %bitcast.45, bf16[]{:T(256)} %constant.131.clone.1), dimensions={0}, to_apply=%region_17.18 | reduce | flops 31948800 | bytes 72417280 | tf_op jit(solution)/shard_map/reduce_sum | solution.py:189
  (323 shorter events, 169.5 us)
Async XLA Ops:
  7.2 48.0 %copy-start = (bf16[48,128,128]{2,1,0:T(8,128)(2,1)S(1)}, bf16[48,128,128]{2,1,0:T(8,128)(2,1)}, u32[]{:S(2)}) copy-start(bf16[48,128,128]{2,1,0:T(8,128)(2,1)} %param.28) | copy-start | bytes 4718596
  8.1 12.7 %copy-start.11 = (s32[16]{0:T(128)}, s32[16]{0:T(128)S(1)}, u32[]{:S(2)}) copy-start(s32[16]{0:T(128)S(1)} %select_reduce_fusion) | copy-start | bytes 196
  32.4 17.1 %copy-start.9 = (s32[16]{0:T(128)S(1)}, s32[16]{0:T(128)}, u32[]{:S(2)}) copy-start(s32[16]{0:T(128)} %param.31) | copy-start | bytes 196
  32.4 18.2 %copy-start.10 = (s32[128]{0:T(128)S(1)}, s32[128]{0:T(128)}, u32[]{:S(2)}) copy-start(s32[128]{0:T(128)} %param.35) | copy-start | bytes 1540
  32.5 20.4 %copy-start.8 = (u32[128]{0:T(128)S(1)}, u32[128]{0:T(128)}, u32[]{:S(2)}) copy-start(u32[128]{0:T(128)} %constant.189) | copy-start | bytes 1540
  36.3 25.3 %all-to-all-start = ((bf16[16,2,15360]{2,1,0:T(2,128)(2,1)}), bf16[16,2,15360]{2,1,0:T(2,128)(2,1)}, u32[]{:S(2)}, u32[]{:S(2)}) async-start(bf16[16,2,15360]{2,1,0:T(2,128)(2,1)} %reshape.374), calls=%async_computation | async-start | bytes 1966080 | tf_op jit(solution)/shard_map/all_to_all | solution.py:73
  61.6 5.9 copy-start.13
  387.3 3.3 copy-start.2
  397.3 4.3 copy-start.3
  397.3 4.3 copy-start.4
  406.4 3.3 copy-start.2
  416.4 4.3 copy-start.3
  416.4 4.3 copy-start.4
  425.4 3.3 copy-start.2
  435.4 4.3 copy-start.3
  435.4 4.3 copy-start.4
  444.4 3.3 copy-start.2
  454.4 4.3 copy-start.3
  454.4 4.3 copy-start.4
  460.3 20.2 %copy-start.6 = (pred[8]{0:T(512)(128)(4,1)S(1)}, pred[8]{0:T(512)(128)(4,1)}, u32[]{:S(2)}) copy-start(pred[8]{0:T(512)(128)(4,1)} %get-tuple-element.149) | copy-start | bytes 28
  462.8 19.2 %copy-start.7 = (pred[4,4]{1,0:T(4,128)(4,1)S(1)}, pred[4,4]{1,0:T(4,128)(4,1)}, u32[]{:S(2)}) copy-start(pred[4,4]{1,0:T(4,128)(4,1)} %broadcast_in_dim.177) | copy-start | bytes 52
  464.6 14.6 %all-to-all-start.1 = ((bf16[16,2,5120]{2,1,0:T(2,128)(2,1)}), bf16[16,2,5120]{2,1,0:T(2,128)(2,1)S(1)}, u32[]{:S(2)}, u32[]{:S(2)}) async-start(bf16[16,2,5120]{2,1,0:T(2,128)(2,1)} %reshape.376), calls=%async_computation.1 | async-start | bytes 655360 | tf_op jit(solution)/shard_map/all_to_all | solution.py:157
  471.3 95.8 %all-gather.7.cloned.1.call-start = ((), (), s32[]{:S(2)}) async-start(), calls=%async_computation.3 | async-start | bytes 5013504 | tf_op jit(solution)/shard_map/all_gather | solution.py:185
  483.0 30.9 %copy-start.5 = (f32[2048]{0:T(1024)S(1)}, f32[2048]{0:T(1024)}, u32[]{:S(2)}) copy-start(f32[2048]{0:T(1024)} %param.25) | copy-start | bytes 24580
  506.3 6.8 collective-permute-start
  514.8 446.3 %all-gather.5.cloned.1.call-start = ((), (), s32[]{:S(2)}) async-start(), calls=%async_computation.2 | async-start | bytes 72417280 | tf_op jit(solution)/shard_map/all_gather | solution.py:190
  571.6 5.7 copy-start.12
  961.1 27.1 %copy-start.1 = (bf16[48,128,128]{2,1,0:T(8,128)(2,1)S(1)}, bf16[48,128,128]{2,1,0:T(8,128)(2,1)}, u32[]{:S(2)}) copy-start(bf16[48,128,128]{2,1,0:T(8,128)(2,1)} %param.28) | copy-start | bytes 4718596
Sparse Core Ops, SparseCore 0:
  514.9 52.1 all-gather.6
  587.4 373.5 all-gather.4
